TPU v7x, 32 devices: a whole 2x2x4 slice. The times are simulated.
32 devices in a mesh: expert: 16 (over z, x, core), tensor: 2 (over y).
Axes of the slice: x: 2, y: 2, z: 4, core: 2. Of those that a mesh axis runs over, the one named last changes fastest.
Arguments:
- grad_out: bfloat16 [2048, 4096], P('expert', 'tensor'), may hold values from -1 to 1
- routes: int32 [2048, 6], P('expert'), may hold values from 0 to 15, all different within a row; in each aligned block of 128 rows (0 to 127, 128 to 255, ...) at most 96 rows name the same one
- scores: float32 [2048, 6], P('expert'), may hold values from -6 to 6
- hidden_act: bfloat16 [16, 1536, 1408], P('expert', None, 'tensor'), may hold values from -6 to 6
- w_down: bfloat16 [16, 1408, 4096], P('expert', 'tensor'), may hold values from -0.15625 to 0.15625
Outputs:
- d_hidden: bfloat16 [16, 1536, 1408], P('expert', None, 'tensor')
- grad_w: bfloat16 [16, 1408, 4096], P('expert', 'tensor')
- grad_scores: float32 [2048, 6], P('expert')
Inputs may be any that keep to these rules, and one draw needn't show every extreme that they name: `routes`: each row names 6 different experts. In each aligned block of 128 rows no expert is named by more than 96 rows, a bound that some block reaches.
All inputs are finite; a program needn't handle non-finite values.
Results may differ from a plain program's by a relative error of at most 0.012.
Values may be sent and summed in bfloat16 or wider, within the bound.
A program may use at most 128 MiB of HBM per device.

v0:
```python
import jax
import jax.numpy as jnp
from jax import lax
from jax.sharding import PartitionSpec as P


def shards(grad_out, routes, scores, hidden_act, w_down):
    expert_count = lax.axis_size("expert")
    tok_rows = routes.shape[0]
    top_count = routes.shape[1]
    slot_count = hidden_act.shape[1]
    per_source = slot_count // expert_count
    flat_routes = routes.reshape(-1)
    onehot = (flat_routes[:, None] == jnp.arange(expert_count, dtype=jnp.int32)[None, :]).astype(
        jnp.int32
    )
    slot_rank = jnp.sum((jnp.cumsum(onehot, axis=0) - onehot) * onehot, axis=1)
    slot_place = flat_routes * per_source + slot_rank
    gates = jax.nn.sigmoid(scores)
    gate_sum = jnp.sum(gates, axis=1, keepdims=True)
    probs = gates / gate_sum
    token_ids = jnp.arange(tok_rows * top_count, dtype=jnp.int32) // top_count
    slot_owner = (
        jnp.full((expert_count * per_source,), tok_rows, jnp.int32).at[slot_place].set(token_ids)
    )
    slot_probs = (
        jnp.zeros((expert_count * per_source,), jnp.float32).at[slot_place].set(probs.reshape(-1))
    )
    saved_act = hidden_act[0]
    down_rows = w_down[0]
    outgoing = jnp.take(grad_out, slot_owner, axis=0, mode="fill", fill_value=0).reshape(
        expert_count, per_source, -1
    )
    narrow, slot_weight = (
        lax.all_to_all(outgoing, "expert", split_axis=0, concat_axis=0, tiled=True),
        lax.all_to_all(
            slot_probs.reshape(expert_count, per_source).astype(jnp.bfloat16),
            "expert",
            split_axis=0,
            concat_axis=0,
            tiled=True,
        ).astype(jnp.float32),
    )
    narrow = narrow.reshape(slot_count, -1)
    slot_weight = slot_weight.reshape(slot_count)
    segment = lax.all_gather(narrow, "tensor", axis=1, tiled=True)
    proj_sum = lax.dot_general(
        segment, down_rows, (((1,), (1,)), ((), ())), preferred_element_type=jnp.float32
    )
    scaled = (segment * slot_weight[:, None]).astype(jnp.bfloat16)
    fresh = lax.dot_general(
        saved_act, scaled, (((0,), (0,)), ((), ())), preferred_element_type=jnp.float32
    )
    partial_value = jnp.sum(proj_sum * saved_act.astype(jnp.float32), axis=1)
    hidden_grad = (slot_weight[:, None] * proj_sum).astype(jnp.bfloat16)
    summed = lax.psum(partial_value, "tensor")
    returned = lax.all_to_all(
        summed.reshape(expert_count, per_source), "expert", split_axis=0, concat_axis=0, tiled=True
    )
    prob_grad = returned.reshape(-1)[slot_place].reshape(tok_rows, top_count)
    mean_term = jnp.sum(probs * prob_grad, axis=1, keepdims=True)
    grad_scores = gates * (1.0 - gates) * (prob_grad - mean_term) / gate_sum
    return (hidden_grad[None], fresh.astype(jnp.bfloat16)[None], grad_scores)


def solution(mesh):
    return jax.shard_map(
        shards,
        mesh=mesh,
        in_specs=(
            P("expert", "tensor"),
            P("expert", None),
            P("expert", None),
            P("expert", None, "tensor"),
            P("expert", "tensor", None),
        ),
        out_specs=(P("expert", None, "tensor"), P("expert", "tensor", None), P("expert", None)),
        check_vma=False,
    )
```

profile of v0, /device:TPU:0, one launch (start us, length us, event | category | flops | bytes accessed | tf_op | source)
XLA Modules:
  0.0 401.2 jit_solution(332698810590436367)
XLA Ops:
  7.2 0.8 copy.22
  8.1 0.1 eq.29
  8.2 0.1 eq.25
  8.3 0.7 broadcast_multiply_fusion
  9.1 1.7 reduce-window.6
  10.8 0.3 slice_reduce_fusion
  11.1 0.1 copy.21
  11.2 0.1 mul.49
  11.3 0.1 fusion.10
  11.4 3.4 scatter_custom_fusion.1
  15.0 7.1 %gather_fusion = bf16[1536,2048]{1,0:T(8,128)(2,1)} fusion(bf16[128,2048]{1,0:T(8,128)(2,1)S(1)} %copy-done, s32[2048]{0:T(1024)S(1)} %pad_clamp_fusion), kind=kCustom, calls=%fused_computation | custom fusion | bytes 12589056 | tf_op jit(solution)/shard_map/jit(_take)/gather | solution.py:31
  22.1 3.3 broadcast_select_fusion
  25.3 144.3 %all_to_all.20 = bf16[16,96,2048]{2,1,0:T(8,128)(2,1)} all-to-all(bf16[16,96,2048]{2,1,0:T(8,128)(2,1)S(1)} %broadcast_select_fusion), channel_id=1, replica_groups=mesh['expert'=16,'tensor'=2] {'expert'}, dimensions={0} | all-to-all | bytes 12582912 | tf_op jit(solution)/shard_map/all_to_all | solution.py:35
  169.7 0.7 copy-done.1
  170.4 152.9 %all-gather.2.cloned.1.call-done = bf16[1536,4096]{1,0:T(8,128)(2,1)} async-done(((bf16[1536,2048]{1,0:T(8,128)(2,1)}), bf16[1536,4096]{1,0:T(8,128)(2,1)}) %all-gather.2.cloned.1.call-update) | async-done | bytes 12582928 | tf_op jit(solution)/shard_map/all_gather | solution.py:46
  323.3 15.2 %multiply_reduce_fusion = (f32[1536]{0:T(1024)S(1)}, f32[1536,704]{0,1:T(8,128)}) fusion(bf16[1,1536,704]{1,2,0:T(8,128)(2,1)S(1)} %copy-done.2, bf16[1536,4096]{1,0:T(8,128)(2,1)} %all-gather.2.cloned.1.call-done, bf16[1,704,4096]{2,1,0:T(8,128)(2,1)} %param.9), kind=kOutput, calls=%fused_computation.12 | convolution fusion | flops 8861612032 | bytes 24844288 | tf_op jit(solution)/shard_map/dot_general | solution.py:47
  338.5 5.6 %psum.7 = f32[16,1,96]{2,1,0:T(1,128)} all-reduce(f32[16,1,96]{2,1,0:T(1,128)S(1)} %all_to_all.15), channel_id=1, replica_groups=mesh['expert'=16,'tensor'=2] {'tensor'}, use_global_device_ids=true, to_apply=%region_7.8 | all-reduce | flops 1536 | bytes 12288 | tf_op jit(solution)/shard_map/psum | solution.py:56
  344.1 5.6 %all-to-all-start.2 = ((f32[16,1,96]{2,1,0:T(1,128)}), f32[16,1,96]{2,1,0:T(1,128)S(1)}, u32[]{:S(2)}, u32[]{:S(2)}) async-start(f32[16,1,96]{2,1,0:T(1,128)} %psum.7), calls=%async_computation.2 | async-start | bytes 16384 | tf_op jit(solution)/shard_map/all_to_all | solution.py:57
  349.7 6.3 %all-to-all-done.2 = f32[16,1,96]{2,1,0:T(1,128)S(1)} async-done(((f32[16,1,96]{2,1,0:T(1,128)}), f32[16,1,96]{2,1,0:T(1,128)S(1)}, u32[]{:S(2)}, u32[]{:S(2)}) %all-to-all-start.2) | async-done | bytes 6176 | tf_op jit(solution)/shard_map/all_to_all | solution.py:57
  356.1 0.5 broadcast.90
  356.6 0.7 reduce.11
  357.3 4.5 %gather_fusion.1 = f32[768]{0:T(1024)S(1)} fusion(f32[1536]{0:T(1024)S(1)} %reshape.107, s32[1024]{0:T(1024)S(1)} %pad_clamp_fusion.1), kind=kCustom, calls=%fused_computation.1 | custom fusion | bytes 9216 | tf_op jit(solution)/shard_map/gather | solution.py:60
  361.8 0.1 reshape.108
  362.1 0.1 copy.25
  362.2 0.1 reshape.130
  362.3 3.4 scatter_custom_fusion
  365.7 0.7 convert_element_type.61
  366.4 3.7 all-to-all-start
  370.1 0.6 fusion.13
  370.7 5.5 %all-to-all-done = bf16[16,1,96]{2,1,0:T(2,128)(2,1)S(1)} async-done(((bf16[16,1,96]{2,1,0:T(2,128)(2,1)}), bf16[16,1,96]{2,1,0:T(2,128)(2,1)S(1)}, u32[]{:S(2)}, u32[]{:S(2)}) %all-to-all-start) | async-done | bytes 3104 | tf_op jit(solution)/shard_map/all_to_all | solution.py:36
  376.3 4.1 %fusion.6 = bf16[1,1536,704]{1,2,0:T(8,128)(2,1)} fusion(f32[1536,704]{0,1:T(8,128)} %get-tuple-element.12, f32[1536]{0:T(1024)S(1)} %reshape.109), kind=kLoop, calls=%fused_computation.14 | loop fusion | flops 2162688 | bytes 6494208 | tf_op jit(solution)/shard_map/broadcast_in_dim | solution.py:63
  380.4 14.0 %fusion.3 = bf16[1,704,4096]{2,1,0:T(8,128)(2,1)} fusion(bf16[1536,4096]{1,0:T(8,128)(2,1)} %all-gather.2.cloned.1.call-done, f32[1536]{0:T(1024)S(1)} %reshape.109, bf16[1,1536,704]{1,2,0:T(8,128)(2,1)S(1)} %copy-done.2), kind=kOutput, calls=%fused_computation.9 | convolution fusion | flops 8880128000 | bytes 20518912 | tf_op jit(solution)/shard_map/dot_general | solution.py:51
  (24 shorter events, 0.6 us)
Async XLA Ops:
  7.2 7.8 %copy-start = (bf16[128,2048]{1,0:T(8,128)(2,1)S(1)}, bf16[128,2048]{1,0:T(8,128)(2,1)}, u32[]{:S(2)}) copy-start(bf16[128,2048]{1,0:T(8,128)(2,1)} %param.5) | copy-start | bytes 1572868
  7.2 316.1 %all-gather.2.cloned.1.call-start = ((), (), s32[]{:S(2)}) async-start(), calls=%async_computation.3 | async-start | bytes 18874368 | tf_op jit(solution)/shard_map/all_gather | solution.py:46
  169.7 0.7 copy-start.1
  169.7 153.6 %copy-start.2 = (bf16[1,1536,704]{1,2,0:T(8,128)(2,1)S(1)}, bf16[1,1536,704]{1,2,0:T(8,128)(2,1)}, u32[]{:S(2)}) copy-start(bf16[1,1536,704]{1,2,0:T(8,128)(2,1)} %param.8) | copy-start | bytes 6488068
  344.1 12.0 %all-to-all-start.2 = ((f32[16,1,96]{2,1,0:T(1,128)}), f32[16,1,96]{2,1,0:T(1,128)S(1)}, u32[]{:S(2)}, u32[]{:S(2)}) async-start(f32[16,1,96]{2,1,0:T(1,128)} %psum.7), calls=%async_computation.2 | async-start | bytes 16384 | tf_op jit(solution)/shard_map/all_to_all | solution.py:57
  366.4 9.8 %all-to-all-start = ((bf16[16,1,96]{2,1,0:T(2,128)(2,1)}), bf16[16,1,96]{2,1,0:T(2,128)(2,1)S(1)}, u32[]{:S(2)}, u32[]{:S(2)}) async-start(bf16[16,1,96]{2,1,0:T(2,128)(2,1)} %convert_element_type.61), calls=%async_computation | async-start | bytes 16384 | tf_op jit(solution)/shard_map/all_to_all | solution.py:36
Sparse Core Ops, SparseCore 0:
  169.8 153.3 all-gather.1
where the time goes:
time: 402 us; the launch traced here: 401 us
  waiting for transfers between devices  165 us (41%)
  blocking collectives  150 us (37%)
  matrix products  29.2 us (7%)
  local copies, waits for them, and re-layouts  22.5 us (6%)
  between operations  14.2 us (4%)
  other arithmetic  11.3 us (3%)
  starting transfers between devices  9.31 us (2%)
    all_gather x1, waiting for transfers between devices, shards(): segment = lax.all_gather(narrow, 'tensor', axis=1, tiled=True)  153 us
    all_to_all x1, blocking collectives, shards(): lax.all_to_all(outgoing, 'expert', split_axis=0, concat_axis=0, tiled=True)  144 us
    dot_general x1, matrix products, shards(): lax.dot_general(segment, down_rows, (((1,), (1,)), ((), ())), preferred_e...  15.2 us
    dot_general x1, matrix products, shards(): lax.dot_general(saved_act, scaled, (((0,), (0,)), ((), ())), preferred_el...  14 us
  transfers between devices with their start and end apart: 3, of which 3 were waited for; matrix products, arithmetic and copies ran while one was open for 0% of the time, Pallas kernels for 0%

commit v1 on v0

--- a/solution.py
+++ b/solution.py
@@ -1,7 +1,381 @@
+import functools
+
 import jax
 import jax.numpy as jnp
 from jax import lax
+from jax.experimental import pallas as pl
+from jax.experimental.pallas import tpu as pltpu
 from jax.sharding import PartitionSpec as P
+
+MESH = pl.DeviceIdType.MESH
+NT = (((1,), (1,)), ((), ()))
+TN = (((0,), (0,)), ((), ()))
+VMEM_BYTES = 67_000_000
+
+
+def item_order(ranks):
+    items = [(k, a, b) for k in range(ranks) for a in (0, 1) for b in (0, 1)]
+    return sorted(items, key=lambda i: (i[0] + i[1] * 0.9 + i[2] * (1.2 + 0.5 * i[0] + 0.3 * i[1]), i))
+
+
+def kernel(
+    dims,
+    pm_ref,
+    g_ref,
+    h_ref,
+    w_ref,
+    dh_ref,
+    gw_ref,
+    pd_ref,
+    G,
+    W,
+    H,
+    HT,
+    HpT,
+    sel,
+    acc,
+    obuf,
+    dhb,
+    bpt,
+    pr,
+    pgs,
+    pgr,
+    rs,
+    sa,
+    sb,
+    sz,
+    sp,
+    pss,
+    prs,
+    gss,
+    grs,
+    ls,
+    os_,
+    ds_,
+):
+    nz, tok, feat, hid, slots = dims
+    n_exp = nz * 4
+    group = 4 * tok
+    quarter = tok // 4
+    pieces = ((0, tok - quarter, 1), (tok - quarter, quarter, 2))
+    e = lax.axis_index("expert")
+    y = lax.axis_index("tensor")
+    z, x, c = e // 4, (e // 2) % 2, e % 2
+
+    tables = [sorted(range(nz), key=lambda o: (abs(o - i), o)) for i in range(nz)]
+
+    def ranked(k):
+        val = jnp.int32(0)
+        for i in range(nz):
+            val = val + jnp.where(z == i, jnp.int32(tables[i][k]), jnp.int32(0))
+        return val
+
+    zk = [ranked(k) for k in range(nz)]
+
+    def dev(z_, x_, y_, c_):
+        return ((z_ * 2 + x_) * 2 + c_, y_)
+
+    load_g = pltpu.make_async_copy(g_ref, G.at[z, y, pl.ds((x * 2 + c) * tok, tok), :], ls.at[0])
+    load_h = pltpu.make_async_copy(h_ref, H, ls.at[1])
+    load_w = pltpu.make_async_copy(w_ref, W, ls.at[2])
+    load_g.start()
+    load_h.start()
+    load_w.start()
+
+    barrier = pltpu.get_barrier_semaphore()
+    total = n_exp * 2
+    lin = e * 2 + y
+
+    def greet(i, carry):
+        to = (lin + i) % total
+        pl.semaphore_signal(barrier, inc=1, device_id=(to // 2, to % 2), device_id_type=MESH)
+        return carry
+
+    lax.fori_loop(1, total, greet, 0)
+    pl.semaphore_wait(barrier, total - 1)
+
+    partner = dev(z, x, y, 1 - c)
+    a_dev = dev(z, (x + 1 - c) % 2, (y + c) % 2, c)
+    b_dev = dev(z, (x + c) % 2, (y + 1 - c) % 2, c)
+    up_dev = dev(jnp.minimum(z + 1, nz - 1), x, y, c)
+    down_dev = dev(jnp.maximum(z - 1, 0), x, y, c)
+
+    def place(k, a, b, color, piece):
+        fx = a * (1 - color) + b * color
+        fy = a * color + b * (1 - color)
+        x_, y_ = (x + fx) % 2, (y + fy) % 2
+        row, rows, _ = pieces[piece]
+        ref = G.at[zk[k], y_, pl.ds((x_ * 2 + color) * tok + row, rows), :]
+        return ref, rs.at[zk[k], x_ * 2 + color, y_, piece]
+
+    def send(ref, recv, sem, to):
+        pltpu.make_async_remote_copy(ref, ref, sem, recv, device_id=to, device_id_type=MESH).start()
+
+    def await_piece(ref, recv):
+        pltpu.make_async_remote_copy(ref, ref, sp, recv, device_id=partner, device_id_type=MESH).wait_recv()
+
+    def handle(k, a, b):
+        for piece in range(len(pieces)):
+            kind = pieces[piece][2]
+            ref, recv = place(k, a, b, c, piece)
+            if (k, a, b) != (0, 0, 0):
+                await_piece(ref, recv)
+            if (a, b) == (0, 0) or kind == 2:
+
+                @pl.when(jnp.logical_and(zk[k] <= z, z < nz - 1))
+                def _():
+                    send(ref, recv, sz.at[0, zk[k]], up_dev)
+
+                @pl.when(jnp.logical_and(zk[k] >= z, z > 0))
+                def _():
+                    send(ref, recv, sz.at[1, zk[k]], down_dev)
+
+            if (a, b) == (0, 0) and (kind == 1 or k == 0):
+                send(ref, recv, sa, a_dev)
+            if b == 0 and (kind == 1 or k == 0):
+                send(ref, recv, sb, b_dev)
+            send(ref, recv, sp, partner)
+
+    load_g.wait()
+    handle(0, 0, 0)
+
+    def send_p(i, carry):
+        to = (e + i) % n_exp
+        pltpu.make_async_remote_copy(
+            pm_ref.at[to], pr.at[e], pss.at[to], prs.at[e], device_id=(to, y), device_id_type=MESH
+        ).start()
+        return carry
+
+    lax.fori_loop(1, n_exp, send_p, 0)
+    pr[e] = pm_ref[e]
+
+    def wait_p(i, carry):
+        frm = (e + i) % n_exp
+        copy = pltpu.make_async_remote_copy(
+            pm_ref.at[frm], pr.at[frm], pss.at[frm], prs.at[frm], device_id=(frm, y), device_id_type=MESH
+        )
+        copy.wait_recv()
+        copy.wait_send()
+        return carry
+
+    lax.fori_loop(1, n_exp, wait_p, 0)
+    load_h.wait()
+    before = (
+        lax.broadcasted_iota(jnp.int32, (tok, tok), 0) < lax.broadcasted_iota(jnp.int32, (tok, tok), 1)
+    ).astype(jnp.bfloat16)
+    slot_ids = lax.broadcasted_iota(jnp.int32, (slots, tok), 0).astype(jnp.float32)
+
+    def prepare(line, carry):
+        for j in range(4):
+            p = pr[line * 4 + j]
+            routed = (p > 0.0).astype(jnp.float32)
+            rank = jnp.dot(routed.astype(jnp.bfloat16), before, preferred_element_type=jnp.float32)
+            rank = jnp.where(p > 0.0, rank, -1.0)
+            pick = (slot_ids == rank[0:1, :]).astype(jnp.float32).astype(jnp.bfloat16)
+            sel[line * 4 + j] = pick
+            rows = H[pl.ds(pl.multiple_of((line * 4 + j) * slots, 16), slots), :]
+            ht = lax.dot_general(rows, pick, TN, preferred_element_type=jnp.float32)
+            HT[line, :, j * tok : (j + 1) * tok] = ht.astype(jnp.bfloat16)
+            HpT[line, :, j * tok : (j + 1) * tok] = (ht * p[0:1, :]).astype(jnp.bfloat16)
+        return carry
+
+    lax.fori_loop(0, nz, prepare, 0)
+
+    def await_partner(k):
+        for a in (0, 1):
+            for b in (0, 1):
+                for piece in range(len(pieces)):
+                    await_piece(*place(k, a, b, 1 - c, piece))
+
+    def project(k, half):
+        line = zk[k]
+        cols = slice(half * 2 * tok, (half + 1) * 2 * tok)
+        bpt[...] = lax.dot_general(
+            W[:, :feat], G[line, 0, cols, :], NT, preferred_element_type=jnp.float32
+        ) + lax.dot_general(W[:, feat:], G[line, 1, cols, :], NT, preferred_element_type=jnp.float32)
+        for i in range(2):
+            j = half * 2 + i
+            block = line * 4 + j
+            back = bpt[:, i * tok : (i + 1) * tok]
+            value = jnp.sum(
+                back * HT[line, :, j * tok : (j + 1) * tok].astype(jnp.float32), axis=0, keepdims=True
+            )
+            pgs[block] = jnp.broadcast_to(value, (8, tok))
+            scaled = (back * pr[block][0:1, :]).astype(jnp.bfloat16)
+            dhb[pl.ds(pl.multiple_of(block * slots, 16), slots), :] = lax.dot_general(
+                sel[block], scaled, NT, preferred_element_type=jnp.float32
+            ).astype(jnp.bfloat16)
+
+    def send_values(k):
+        line = zk[k]
+        for j in range(4):
+            block = line * 4 + j
+            for y_ in range(2):
+
+                @pl.when(jnp.logical_or(block != e, y != y_))
+                def _():
+                    pltpu.make_async_remote_copy(
+                        pgs.at[block],
+                        pgr.at[y, e],
+                        gss.at[y_, block],
+                        grs.at[y, e],
+                        device_id=(block, y_),
+                        device_id_type=MESH,
+                    ).start()
+
+        rows = pl.ds(pl.multiple_of(line * 4 * slots, 16), 4 * slots)
+        pltpu.make_async_copy(dhb.at[rows, :], dh_ref.at[rows, :], ds_.at[k]).start()
+
+    width = feat // 4
+
+    def weigh(k, half):
+        line = zk[k]
+
+        def one(n, carry):
+            cols = pl.ds(pl.multiple_of(n * width, width), width)
+            dest = pl.ds(pl.multiple_of(half * feat + n * width, width), width)
+            part = jnp.dot(HpT[line], G[line, half, :, cols], preferred_element_type=jnp.float32)
+            if k == 0:
+                acc[:, dest] = part
+            elif k < nz - 1:
+                acc[:, dest] += part
+            else:
+                obuf[:, dest] = (acc[:, dest] + part).astype(jnp.bfloat16)
+                pltpu.make_async_copy(obuf.at[:, dest], gw_ref.at[:, dest], os_.at[half * 4 + n]).start()
+            return carry
+
+        lax.fori_loop(0, 4, one, 0)
+
+    units = []
+    for k in range(nz):
+        units.append((k, lambda k=k: (await_partner(k), project(k, 0))))
+        units.append((k, lambda k=k: (project(k, 1), send_values(k))))
+        units.append((k, lambda k=k: weigh(k, 0)))
+        units.append((k, lambda k=k: weigh(k, 1)))
+
+    order = item_order(nz)[1:]
+    done = {k: 1 if k == 0 else 0 for k in range(nz)}
+    started = False
+    for item in order:
+        handle(*item)
+        done[item[0]] += 1
+        if units and done[units[0][0]] == 4:
+            if not started:
+                load_w.wait()
+                started = True
+            units.pop(0)[1]()
+    for _, unit in units:
+        unit()
+
+    pgr[y, e] = pgs[e]
+
+    def settle(i, carry):
+        at = (lin + i) % total
+        e_, y_ = at // 2, at % 2
+        copy = pltpu.make_async_remote_copy(
+            pgs.at[e_], pgr.at[y_, e_], gss.at[y_, e_], grs.at[y_, e_], device_id=(e_, y_), device_id_type=MESH
+        )
+        copy.wait_recv()
+        copy.wait_send()
+        return carry
+
+    lax.fori_loop(1, total, settle, 0)
+    pd_ref[...] = pgr[0] + pgr[1]
+
+    def await_sent(ref, sem):
+        pltpu.make_async_remote_copy(ref, ref, sem, rs.at[0, 0, 0, 0], device_id=partner, device_id_type=MESH).wait_send()
+
+    wide = tok - quarter
+    await_sent(G.at[0, 0, pl.ds(0, nz * wide + quarter), :], sa)
+    await_sent(G.at[0, :, pl.ds(0, nz * wide + quarter), :], sb)
+    await_sent(G.at[:, 0], sp)
+    for k in range(nz):
+
+        @pl.when(jnp.logical_and(zk[k] <= z, z < nz - 1))
+        def _():
+            await_sent(G.at[0, 0, pl.ds(0, wide + 4 * quarter), :], sz.at[0, zk[k]])
+
+        @pl.when(jnp.logical_and(zk[k] >= z, z > 0))
+        def _():
+            await_sent(G.at[0, 0, pl.ds(0, wide + 4 * quarter), :], sz.at[1, zk[k]])
+
+    for k in range(nz):
+        rows = pl.ds(pl.multiple_of(zk[k] * 4 * slots, 16), 4 * slots)
+        pltpu.make_async_copy(dhb.at[rows, :], dh_ref.at[rows, :], ds_.at[k]).wait()
+    for n in range(8):
+        dest = pl.ds(n * width, width)
+        pltpu.make_async_copy(obuf.at[:, dest], gw_ref.at[:, dest], os_.at[n]).wait()
+
+
+def fused_shards(grad_out, routes, scores, hidden_act, w_down):
+    n_exp = lax.axis_size("expert")
+    nz = n_exp // 4
+    tok, feat = grad_out.shape
+    slot_count, hid = hidden_act.shape[1:]
+    slots = slot_count // n_exp
+    experts = jnp.arange(n_exp, dtype=jnp.int32)
+    gates = jax.nn.sigmoid(scores)
+    gate_sum = jnp.sum(gates, axis=1, keepdims=True)
+    probs = gates / gate_sum
+    onehot = routes[None, :, :] == experts[:, None, None]
+    dense = jnp.sum(jnp.where(onehot, probs[None], 0.0), axis=2)
+    pm = jnp.broadcast_to(dense[:, None, :], (n_exp, 8, tok))
+    bf, f32 = jnp.bfloat16, jnp.float32
+    dma = pltpu.SemaphoreType.DMA
+    d_hidden, grad_w, pd = pl.pallas_call(
+        functools.partial(kernel, (nz, tok, feat, hid, slots)),
+        out_shape=(
+            jax.ShapeDtypeStruct((slot_count, hid), bf),
+            jax.ShapeDtypeStruct((hid, 2 * feat), bf),
+            jax.ShapeDtypeStruct((n_exp, 8, tok), f32),
+        ),
+        in_specs=[
+            pl.BlockSpec(memory_space=pltpu.VMEM),
+            pl.BlockSpec(memory_space=pl.ANY),
+            pl.BlockSpec(memory_space=pl.ANY),
+            pl.BlockSpec(memory_space=pl.ANY),
+        ],
+        out_specs=(
+            pl.BlockSpec(memory_space=pl.ANY),
+            pl.BlockSpec(memory_space=pl.ANY),
+            pl.BlockSpec(memory_space=pltpu.VMEM),
+        ),
+        scratch_shapes=[
+            pltpu.VMEM((nz, 2, 4 * tok, feat), bf),
+            pltpu.VMEM((hid, 2 * feat), bf),
+            pltpu.VMEM((slot_count, hid), bf),
+            pltpu.VMEM((nz, hid, 4 * tok), bf),
+            pltpu.VMEM((nz, hid, 4 * tok), bf),
+            pltpu.VMEM((n_exp, slots, tok), bf),
+            pltpu.VMEM((hid, 2 * feat), f32),
+            pltpu.VMEM((hid, 2 * feat), bf),
+            pltpu.VMEM((slot_count, hid), bf),
+            pltpu.VMEM((hid, 2 * tok), f32),
+            pltpu.VMEM((n_exp, 8, tok), f32),
+            pltpu.VMEM((n_exp, 8, tok), f32),
+            pltpu.VMEM((2, n_exp, 8, tok), f32),
+            dma((nz, 4, 2, 2)),
+            dma,
+            dma,
+            dma((2, nz)),
+            dma,
+            dma((n_exp,)),
+            dma((n_exp,)),
+            dma((2, n_exp)),
+            dma((2, n_exp)),
+            dma((3,)),
+            dma((8,)),
+            dma((nz,)),
+        ],
+        compiler_params=pltpu.CompilerParams(
+            collective_id=0, has_side_effects=True, vmem_limit_bytes=VMEM_BYTES
+        ),
+    )(pm, grad_out, hidden_act[0], w_down[0])
+    values = pd[:, 0, :]
+    prob_grad = jnp.sum(jnp.where(onehot, values[:, :, None], 0.0), axis=0)
+    mean_term = jnp.sum(probs * prob_grad, axis=1, keepdims=True)
+    grad_scores = gates * (1.0 - gates) * (prob_grad - mean_term) / gate_sum
+    return d_hidden[None], grad_w[None], grad_scores
 
 
 def shards(grad_out, routes, scores, hidden_act, w_down):
@@ -63,9 +437,13 @@
     return (hidden_grad[None], fresh.astype(jnp.bfloat16)[None], grad_scores)
 
 
+def fits(mesh):
+    return mesh.shape["tensor"] == 2 and mesh.shape["expert"] % 4 == 0 and mesh.shape["expert"] <= 16
+
+
 def solution(mesh):
     return jax.shard_map(
-        shards,
+        fused_shards if fits(mesh) else shards,
         mesh=mesh,
         in_specs=(
             P("expert", "tensor"),

time: 402 us -> 127 us (0.32)
  waiting for transfers between devices: 165 us -> 0 us
  blocking collectives: 150 us -> 0 us
  Pallas kernels: 0 us -> 107 us
  matrix products: 29.2 us -> 0 us
  between operations: 14.2 us -> 0.67 us
  starting transfers between devices: 9.31 us -> 0 us
  other arithmetic: 11.3 us -> 2.78 us
  local copies, waits for them, and re-layouts: 22.5 us -> 15.7 us
    all_gather x1 -> x0, waiting for transfers between devices: 153 us -> none  [shards(): segment = lax.all_gather(narrow, 'tensor', axis=1, tiled=True)]
    all_to_all x1 -> x0, blocking collectives: 144 us -> none  [shards(): lax.all_to_all(outgoing, 'expert', split_axis=0, concat_axis=0, tiled=True)]
    pallas_call x0 -> x1, Pallas kernels: none -> 107 us  [fused_shards(): pl.pallas_call(functools.partial(kernel, (nz, tok, feat, hid, slots)), ou...]
    dot_general x2 -> x0, matrix products: 29.2 us -> none  [the longest x1 15.2 us: shards(): lax.dot_general(segment, down_rows, (((1,), (1,)), ((), ())), preferred_e...]
    unnamed x7, local copies, waits for them, and re-layouts: 1.52 us -> 14.3 us
    all_to_all x2 -> x0, waiting for transfers between devices: 11.9 us -> none  [the longest x1 6.35 us: shards(): lax.all_to_all(summed.reshape(expert_count, per_source), 'expert', split_...]
    gather x2 -> x0, local copies, waits for them, and re-layouts: 11.5 us -> none  [the longest x1 7.09 us: shards(): jnp.take(grad_out, slot_owner, axis=0, mode='fill', fill_value=0)]
    all_to_all x2 -> x0, starting transfers between devices: 9.27 us -> none  [the longest x1 5.62 us: shards(): lax.all_to_all(summed.reshape(expert_count, per_source), 'expert', split_...]
  transfers between devices with their start and end apart: 3 -> 0, of which waited for: 3 -> 0; matrix products, arithmetic and copies ran while one was open for 0% -> 0% of each run, Pallas kernels for 0% -> 0%
where the time goes in v1:
time: 127 us; the launch traced here: 126 us
  Pallas kernels  107 us (84%)
  local copies, waits for them, and re-layouts  15.7 us (12%)
  other arithmetic  2.78 us (2%)
    pallas_call x1, Pallas kernels, fused_shards(): pl.pallas_call(functools.partial(kernel, (nz, tok, feat, hid, slots)), ou...  107 us
    unnamed x7, local copies, waits for them, and re-layouts  14.3 us

profile of v1, /device:TPU:0, one launch (start us, length us, event | category | flops | bytes accessed | tf_op | source)
XLA Modules:
  0.0 126.1 jit_solution(8715077429440738264)
XLA Ops:
  0.6 0.7 fusion.3
  1.3 0.7 multiply_divide_fusion
  2.0 0.7 select_reduce_fusion.1
  2.7 0.6 broadcast_in_dim.43.pm_ref
  3.4 4.2 %copy.12 = bf16[1,1536,704]{2,1,0:T(8,128)(2,1)} copy(bf16[1,1536,704]{1,2,0:T(8,128)(2,1)} %param.8) | data formatting | bytes 4325376 | tf_op args[3]
  7.6 106.9 %shard_map.76 = (bf16[1536,704]{1,0:T(8,128)(2,1)}, bf16[704,4096]{1,0:T(8,128)(2,1)}, f32[16,8,128]{2,1,0:T(8,128)}) custom-call(f32[16,8,128]{2,1,0:T(8,128)} %broadcast_in_dim.43.pm_ref, bf16[128,2048]{1,0:T(8,128)(2,1)} %g_ref.1, bf16[1536,704]{1,0:T(8,128)(2,1)} %bitcast.5, bf16[704,4096]{1,0:T(8,128)(2,1)} %bitcast.6), custom_call_target="tpu_custom_call" | custom-call | tf_op jit(solution)/shard_map/pallas_call | solution.py:325
  114.5 0.0 copy-start.1
  114.5 0.0 copy-start
  114.5 4.2 %copy.13 = bf16[1,1536,704]{1,2,0:T(8,128)(2,1)} copy(bf16[1,1536,704]{2,1,0:T(8,128)(2,1)} %bitcast.8) | data formatting | bytes 4325376
  118.7 0.8 slice.3
  119.5 0.0 copy-done.1
  119.6 0.0 copy-done
  119.6 0.6 fusion.1
  120.2 5.9 %copy.15 = bf16[1,704,4096]{2,1,0:T(8,128)(2,1)} copy(bf16[1,704,4096]{2,1,0:T(8,128)(2,1)} %bitcast.7) | data formatting | bytes 11534336
  (2 shorter events, 0.0 us)
Async XLA Ops:
  114.5 5.1 %copy-start.1 = (s32[128,6]{0,1:T(8,128)S(1)}, s32[128,6]{0,1:T(8,128)}, u32[]{:S(2)}) copy-start(s32[128,6]{0,1:T(8,128)} %param.6) | copy-start | bytes 9220
  114.5 5.1 %copy-start = (f32[128,6]{0,1:T(8,128)S(1)}, f32[128,6]{0,1:T(8,128)}, u32[]{:S(2)}) copy-start(f32[128,6]{0,1:T(8,128)} %param.7) | copy-start | bytes 9220

commit v2 on v1

--- a/solution.py
+++ b/solution.py
@@ -10,7 +10,7 @@
 MESH = pl.DeviceIdType.MESH
 NT = (((1,), (1,)), ((), ()))
 TN = (((0,), (0,)), ((), ()))
-VMEM_BYTES = 67_000_000
+VMEM_BYTES = 57_000_000
 
 
 def item_order(ranks):
@@ -20,13 +20,14 @@
 
 def kernel(
     dims,
-    pm_ref,
+    routes_ref,
+    scores_ref,
     g_ref,
     h_ref,
     w_ref,
-    dh_ref,
-    gw_ref,
-    pd_ref,
+    dhb,
+    obuf,
+    gs_ref,
     G,
     W,
     H,
@@ -34,9 +35,9 @@
     HpT,
     sel,
     acc,
-    obuf,
-    dhb,
+    dht,
     bpt,
+    pm_ref,
     pr,
     pgs,
     pgr,
@@ -50,8 +51,6 @@
     gss,
     grs,
     ls,
-    os_,
-    ds_,
 ):
     nz, tok, feat, hid, slots = dims
     n_exp = nz * 4
@@ -85,6 +84,11 @@
     barrier = pltpu.get_barrier_semaphore()
     total = n_exp * 2
     lin = e * 2 + y
+    top = routes_ref.shape[0]
+    choices = routes_ref[...]
+    gates = jax.nn.sigmoid(scores_ref[...])
+    gate_sum = jnp.sum(gates, axis=0, keepdims=True)
+    probs = gates / gate_sum
 
     def greet(i, carry):
         to = (lin + i) % total
@@ -92,6 +96,9 @@
         return carry
 
     lax.fori_loop(1, total, greet, 0)
+    for ex in range(n_exp):
+        row = jnp.sum(jnp.where(choices == ex, probs, 0.0), axis=0, keepdims=True)
+        pm_ref[ex] = jnp.broadcast_to(row, (8, tok))
     pl.semaphore_wait(barrier, total - 1)
 
     partner = dev(z, x, y, 1 - c)
@@ -163,18 +170,18 @@
     before = (
         lax.broadcasted_iota(jnp.int32, (tok, tok), 0) < lax.broadcasted_iota(jnp.int32, (tok, tok), 1)
     ).astype(jnp.bfloat16)
-    slot_ids = lax.broadcasted_iota(jnp.int32, (slots, tok), 0).astype(jnp.float32)
+    slot_ids = lax.broadcasted_iota(jnp.int32, (4 * slots, tok), 0).astype(jnp.float32)
 
     def prepare(line, carry):
+        cols = pl.ds(pl.multiple_of(line * 4 * slots, 128), 4 * slots)
         for j in range(4):
             p = pr[line * 4 + j]
             routed = (p > 0.0).astype(jnp.float32)
             rank = jnp.dot(routed.astype(jnp.bfloat16), before, preferred_element_type=jnp.float32)
-            rank = jnp.where(p > 0.0, rank, -1.0)
+            rank = jnp.where(p > 0.0, rank + j * slots, -1.0)
             pick = (slot_ids == rank[0:1, :]).astype(jnp.float32).astype(jnp.bfloat16)
-            sel[line * 4 + j] = pick
-            rows = H[pl.ds(pl.multiple_of((line * 4 + j) * slots, 16), slots), :]
-            ht = lax.dot_general(rows, pick, TN, preferred_element_type=jnp.float32)
+            sel[line, :, j * tok : (j + 1) * tok] = pick
+            ht = jnp.dot(H[:, cols], pick, preferred_element_type=jnp.float32)
             HT[line, :, j * tok : (j + 1) * tok] = ht.astype(jnp.bfloat16)
             HpT[line, :, j * tok : (j + 1) * tok] = (ht * p[0:1, :]).astype(jnp.bfloat16)
         return carry
@@ -201,10 +208,7 @@
                 back * HT[line, :, j * tok : (j + 1) * tok].astype(jnp.float32), axis=0, keepdims=True
             )
             pgs[block] = jnp.broadcast_to(value, (8, tok))
-            scaled = (back * pr[block][0:1, :]).astype(jnp.bfloat16)
-            dhb[pl.ds(pl.multiple_of(block * slots, 16), slots), :] = lax.dot_general(
-                sel[block], scaled, NT, preferred_element_type=jnp.float32
-            ).astype(jnp.bfloat16)
+            dht[:, j * tok : (j + 1) * tok] = (back * pr[block][0:1, :]).astype(jnp.bfloat16)
 
     def send_values(k):
         line = zk[k]
@@ -223,8 +227,8 @@
                         device_id_type=MESH,
                     ).start()
 
-        rows = pl.ds(pl.multiple_of(line * 4 * slots, 16), 4 * slots)
-        pltpu.make_async_copy(dhb.at[rows, :], dh_ref.at[rows, :], ds_.at[k]).start()
+        cols = pl.ds(pl.multiple_of(line * 4 * slots, 128), 4 * slots)
+        dhb[:, cols] = lax.dot_general(dht[...], sel[line], NT, preferred_element_type=jnp.float32).astype(jnp.bfloat16)
 
     width = feat // 4
 
@@ -241,7 +245,6 @@
                 acc[:, dest] += part
             else:
                 obuf[:, dest] = (acc[:, dest] + part).astype(jnp.bfloat16)
-                pltpu.make_async_copy(obuf.at[:, dest], gw_ref.at[:, dest], os_.at[half * 4 + n]).start()
             return carry
 
         lax.fori_loop(0, 4, one, 0)
@@ -280,7 +283,11 @@
         return carry
 
     lax.fori_loop(1, total, settle, 0)
-    pd_ref[...] = pgr[0] + pgr[1]
+    wanted = jnp.zeros((top, tok), jnp.float32)
+    for ex in range(n_exp):
+        wanted = wanted + jnp.where(choices == ex, (pgr[0, ex] + pgr[1, ex])[0:1, :], 0.0)
+    mean_term = jnp.sum(probs * wanted, axis=0, keepdims=True)
+    gs_ref[...] = gates * (1.0 - gates) * (wanted - mean_term) / gate_sum
 
     def await_sent(ref, sem):
         pltpu.make_async_remote_copy(ref, ref, sem, rs.at[0, 0, 0, 0], device_id=partner, device_id_type=MESH).wait_send()
@@ -298,13 +305,6 @@
         @pl.when(jnp.logical_and(zk[k] >= z, z > 0))
         def _():
             await_sent(G.at[0, 0, pl.ds(0, wide + 4 * quarter), :], sz.at[1, zk[k]])
-
-    for k in range(nz):
-        rows = pl.ds(pl.multiple_of(zk[k] * 4 * slots, 16), 4 * slots)
-        pltpu.make_async_copy(dhb.at[rows, :], dh_ref.at[rows, :], ds_.at[k]).wait()
-    for n in range(8):
-        dest = pl.ds(n * width, width)
-        pltpu.make_async_copy(obuf.at[:, dest], gw_ref.at[:, dest], os_.at[n]).wait()
 
 
 def fused_shards(grad_out, routes, scores, hidden_act, w_down):
@@ -313,44 +313,38 @@
     tok, feat = grad_out.shape
     slot_count, hid = hidden_act.shape[1:]
     slots = slot_count // n_exp
-    experts = jnp.arange(n_exp, dtype=jnp.int32)
-    gates = jax.nn.sigmoid(scores)
-    gate_sum = jnp.sum(gates, axis=1, keepdims=True)
-    probs = gates / gate_sum
-    onehot = routes[None, :, :] == experts[:, None, None]
-    dense = jnp.sum(jnp.where(onehot, probs[None], 0.0), axis=2)
-    pm = jnp.broadcast_to(dense[:, None, :], (n_exp, 8, tok))
     bf, f32 = jnp.bfloat16, jnp.float32
     dma = pltpu.SemaphoreType.DMA
-    d_hidden, grad_w, pd = pl.pallas_call(
+    d_hidden, grad_w, grad_scores = pl.pallas_call(
         functools.partial(kernel, (nz, tok, feat, hid, slots)),
         out_shape=(
-            jax.ShapeDtypeStruct((slot_count, hid), bf),
-            jax.ShapeDtypeStruct((hid, 2 * feat), bf),
-            jax.ShapeDtypeStruct((n_exp, 8, tok), f32),
+            pltpu.VMEM((hid, slot_count), bf),
+            pltpu.VMEM((hid, 2 * feat), bf),
+            jax.ShapeDtypeStruct(scores.shape[::-1], f32),
         ),
         in_specs=[
+            pl.BlockSpec(memory_space=pltpu.VMEM),
             pl.BlockSpec(memory_space=pltpu.VMEM),
             pl.BlockSpec(memory_space=pl.ANY),
             pl.BlockSpec(memory_space=pl.ANY),
             pl.BlockSpec(memory_space=pl.ANY),
         ],
         out_specs=(
-            pl.BlockSpec(memory_space=pl.ANY),
-            pl.BlockSpec(memory_space=pl.ANY),
+            pl.BlockSpec(memory_space=pltpu.VMEM),
+            pl.BlockSpec(memory_space=pltpu.VMEM),
             pl.BlockSpec(memory_space=pltpu.VMEM),
         ),
         scratch_shapes=[
             pltpu.VMEM((nz, 2, 4 * tok, feat), bf),
             pltpu.VMEM((hid, 2 * feat), bf),
-            pltpu.VMEM((slot_count, hid), bf),
+            pltpu.VMEM((hid, slot_count), bf),
             pltpu.VMEM((nz, hid, 4 * tok), bf),
             pltpu.VMEM((nz, hid, 4 * tok), bf),
-            pltpu.VMEM((n_exp, slots, tok), bf),
+            pltpu.VMEM((nz, 4 * slots, 4 * tok), bf),
             pltpu.VMEM((hid, 2 * feat), f32),
-            pltpu.VMEM((hid, 2 * feat), bf),
-            pltpu.VMEM((slot_count, hid), bf),
+            pltpu.VMEM((hid, 4 * tok), bf),
             pltpu.VMEM((hid, 2 * tok), f32),
+            pltpu.VMEM((n_exp, 8, tok), f32),
             pltpu.VMEM((n_exp, 8, tok), f32),
             pltpu.VMEM((n_exp, 8, tok), f32),
             pltpu.VMEM((2, n_exp, 8, tok), f32),
@@ -364,18 +358,12 @@
             dma((2, n_exp)),
             dma((2, n_exp)),
             dma((3,)),
-            dma((8,)),
-            dma((nz,)),
         ],
         compiler_params=pltpu.CompilerParams(
             collective_id=0, has_side_effects=True, vmem_limit_bytes=VMEM_BYTES
         ),
-    )(pm, grad_out, hidden_act[0], w_down[0])
-    values = pd[:, 0, :]
-    prob_grad = jnp.sum(jnp.where(onehot, values[:, :, None], 0.0), axis=0)
-    mean_term = jnp.sum(probs * prob_grad, axis=1, keepdims=True)
-    grad_scores = gates * (1.0 - gates) * (prob_grad - mean_term) / gate_sum
-    return d_hidden[None], grad_w[None], grad_scores
+    )(routes.T, scores.T, grad_out, hidden_act[0].T, w_down[0])
+    return d_hidden.T[None], grad_w[None], grad_scores.T
 
 
 def shards(grad_out, routes, scores, hidden_act, w_down):

time: 127 us -> 112 us (0.88)
  local copies, waits for them, and re-layouts: 15.7 us -> 4.47 us
  other arithmetic: 2.78 us -> 0 us
    unnamed x7 -> x5, local copies, waits for them, and re-layouts: 14.3 us -> 4.47 us
    reduce_sum x4 -> x0, other arithmetic: 1.46 us -> none  [the longest x1 0.71 us: fused_shards(): gate_sum = jnp.sum(gates, axis=1, keepdims=True)]
    div x2 -> x0, other arithmetic: 1.32 us -> none  [the longest x1 0.7 us: fused_shards(): probs = gates / gate_sum]
where the time goes in v2:
time: 112 us
  Pallas kernels  106 us (95%)
  local copies, waits for them, and re-layouts  4.47 us (4%)
    pallas_call x1, Pallas kernels, fused_shards(): pl.pallas_call(functools.partial(kernel, (nz, tok, feat, hid, slots)), ou...  106 us
    unnamed x5, local copies, waits for them, and re-layouts  4.47 us

profile of v2, /device:TPU:0, one launch (start us, length us, event | category | flops | bytes accessed | tf_op | source)
XLA Modules:
  0.0 111.6 jit_solution(6124339226375347347)
XLA Ops:
  0.6 106.5 %shard_map.76 = (bf16[704,1536]{1,0:T(8,128)(2,1)S(1)}, bf16[704,4096]{1,0:T(8,128)(2,1)S(1)}, f32[6,128]{1,0:T(8,128)}) custom-call(s32[6,128]{1,0:T(8,128)} %bitcast.15, f32[6,128]{1,0:T(8,128)} %bitcast.16, bf16[128,2048]{1,0:T(8,128)(2,1)} %g_ref.1, bf16[704,1536]{1,0:T(8,128)(2,1)} %bitcast.14, bf16[704,4096]{1,0:T(8,128)(2,1)} %bitcast.13), custom_call_target="tpu_custom_call" | custom-call | tf_op jit(solution)/shard_map/pallas_call | solution.py:318
  107.1 1.3 %copy.11 = bf16[1,1536,704]{1,2,0:T(8,128)(2,1)} copy(bf16[1,1536,704]{1,2,0:T(8,128)(2,1)S(1)} %bitcast.12) | data formatting | bytes 4325376
  108.5 0.0 copy-start
  108.5 2.5 %copy.12 = bf16[1,704,4096]{2,1,0:T(8,128)(2,1)} copy(bf16[1,704,4096]{2,1,0:T(8,128)(2,1)S(1)} %bitcast.11) | data formatting | bytes 11534336
  111.0 0.0 copy-done
  111.0 0.6 copy.13
Async XLA Ops:
  108.5 2.5 %copy-start = (f32[6,128]{1,0:T(8,128)S(1)}, f32[6,128]{1,0:T(8,128)}, u32[]{:S(2)}) copy-start(f32[6,128]{1,0:T(8,128)} %get-tuple-element.8) | copy-start | bytes 9220
